TPU v7x, 32 devices: a whole 2x2x4 slice. The times are simulated.
32 devices in a mesh: seq: 8 (over z, x), ep: 4 (over y, core).
Axes of the slice: x: 2, y: 2, z: 4, core: 2. Of those that a mesh axis runs over, the one named last changes fastest.
Arguments:
- tokens: bfloat16 [1024, 2048], P('seq'), may hold values from -12 to 12
- attn_gain: float32 [2048], replicated, may hold values from 0.1 to 1.9
- w_query: bfloat16 [2048, 512], P(None, 'ep'), may hold values from -1 to 1
- w_key: bfloat16 [2048, 512], P(None, 'ep'), may hold values from -8 to 8
- w_value: bfloat16 [2048, 512], P(None, 'ep'), may hold values from -0.125 to 0.125
- w_out: bfloat16 [512, 2048], P('ep'), may hold values from -0.25 to 0.25
- moe_gain: float32 [2048], replicated, may hold values from 0.1 to 1.9
- expert_ids: int32 [1024, 6], P('seq'), may hold values from 0 to 15, all different within a row; in each aligned block of 128 rows (0 to 127, 128 to 255, ...) at most 52 rows name the same one
- route_weight: float32 [1024, 6], P('seq'), may hold values from 0.2 to 1
- w_gate: bfloat16 [5632, 2048], P(('seq', 'ep')), may hold values from -0.125 to 0.125
- w_up: bfloat16 [5632, 2048], P(('seq', 'ep')), may hold values from -0.125 to 0.125
- w_down: bfloat16 [5632, 2048], P(('seq', 'ep')), may hold values from -0.3125 to 0.3125
Outputs:
- layer_out: bfloat16 [1024, 2048], P(('seq', 'ep'))
Inputs may be any that keep to these rules, and one draw needn't show every extreme that they name: `expert_ids`: each frame names 6 different experts; among the frames of one block of 128 no expert is named by more than 52 frames, a bound that some block reaches.
All inputs are finite; a program needn't handle non-finite values.
Results may differ from a plain program's by a relative error of at most 0.0065.
Values may be sent and summed in bfloat16 or wider, within the bound.
A program may use at most 64 MiB of HBM per device.

v0:
```python
import math
import jax
import jax.numpy as jnp
from jax import lax
from jax.sharding import PartitionSpec as P

EXP_ROW = 2
SPAN = 4
epsilon = 1e-05


def shifted(shard, axis, by):
    devices = lax.axis_size(axis)
    pairs = [(i, i + by) for i in range(devices) if 0 <= i + by < devices]
    return lax.ppermute(shard, axis, pairs)


def root_norm(values, gain):
    mean_square = jnp.mean(values * values, axis=-1, keepdims=True)
    return values * lax.rsqrt(mean_square + epsilon) * gain


def body(
    tokens,
    attn_gain,
    w_query,
    w_key,
    w_value,
    w_out,
    moe_gain,
    expert_ids,
    route_weight,
    w_gate,
    w_up,
    w_down,
):
    tok_rows, model_width = tokens.shape
    head_size = w_query.shape[1]
    seq_count = lax.axis_size("seq")
    ep_count = lax.axis_size("ep")
    seq_place = lax.axis_index("seq")
    ep_place = lax.axis_index("ep")
    row_share = tok_rows // ep_count
    tok_float = tokens.astype(jnp.float32)
    normed = root_norm(tok_float, attn_gain).astype(jnp.bfloat16)
    query_vectors = jnp.dot(normed, w_query, preferred_element_type=jnp.float32).astype(
        jnp.bfloat16
    )
    keys = jnp.dot(normed, w_key, preferred_element_type=jnp.float32).astype(jnp.bfloat16)
    values = jnp.dot(normed, w_value, preferred_element_type=jnp.float32).astype(jnp.bfloat16)
    stacked = jnp.stack([keys, values])
    key_parts = []
    value_parts = []
    for distance in range(SPAN, 0, -1):
        earlier = shifted(stacked, "seq", distance)
        key_parts.append(earlier[0])
        value_parts.append(earlier[1])
    window_key_rows = jnp.concatenate(key_parts + [keys], axis=0)
    window_value_rows = jnp.concatenate(value_parts + [values], axis=0)
    attention_logits = lax.dot_general(
        query_vectors, window_key_rows, (((1,), (1,)), ((), ())), preferred_element_type=jnp.float32
    ) / math.sqrt(head_size)
    query_pos = jnp.arange(tok_rows, dtype=jnp.int32)[:, None]
    key_rel = jnp.arange((SPAN + 1) * tok_rows, dtype=jnp.int32)[None, :] - SPAN * tok_rows
    window_len = SPAN * tok_rows
    allowed = (
        (key_rel <= query_pos)
        & (key_rel > query_pos - window_len)
        & (seq_place * tok_rows + key_rel >= 0)
    )
    attention_logits = jnp.where(allowed, attention_logits, -1e30)
    peak = jnp.max(attention_logits, axis=-1, keepdims=True)
    expo = jnp.exp(attention_logits - peak)
    attention_probabilities = (expo / jnp.sum(expo, axis=-1, keepdims=True)).astype(jnp.bfloat16)
    attention_output = jnp.dot(
        attention_probabilities, window_value_rows, preferred_element_type=jnp.float32
    ).astype(jnp.bfloat16)
    head_terms = jnp.dot(attention_output, w_out, preferred_element_type=jnp.float32)
    attn_total = lax.psum(head_terms, "ep")
    residual = tok_float + attn_total
    moe_in = root_norm(residual, moe_gain).astype(jnp.bfloat16)
    resid_rows = lax.dynamic_slice_in_dim(residual, ep_place * row_share, row_share, 0)
    top_count = expert_ids.shape[1]
    experts_all = seq_count * EXP_ROW
    slices = ep_count // EXP_ROW
    expert_half = ep_place // slices
    capacity = tok_rows * top_count // experts_all + tok_rows // 32
    expert_iota = jnp.arange(experts_all, dtype=jnp.int32)
    chosen = (expert_ids[:, :, None] == expert_iota).astype(jnp.float32)
    counts = jnp.sum(chosen, axis=1)
    earlier_mask = (jnp.arange(tok_rows)[:, None] > jnp.arange(tok_rows)[None, :]).astype(
        jnp.float32
    )
    before = jnp.dot(
        earlier_mask, counts, precision=lax.Precision.HIGHEST, preferred_element_type=jnp.float32
    )
    slot_index = jnp.sum(chosen * before[:, None, :], axis=-1)
    own_pairs = expert_ids % EXP_ROW == expert_half
    flat_slot = (expert_ids // EXP_ROW).astype(jnp.float32) * capacity + slot_index
    slot_iota = jnp.arange(seq_count * capacity, dtype=jnp.float32)
    slot_hits = (flat_slot[:, :, None] == slot_iota) & own_pairs[:, :, None]
    dispatch = jnp.any(slot_hits, axis=1).astype(jnp.bfloat16)
    panels = lax.dot_general(
        dispatch, moe_in, (((0,), (0,)), ((), ())), preferred_element_type=jnp.float32
    )
    panels = panels.astype(jnp.bfloat16).reshape(seq_count, capacity, model_width)
    rate = route_weight.astype(jnp.bfloat16).astype(jnp.float32)
    combine = jnp.sum(jnp.where(slot_hits, rate[:, :, None], 0.0), axis=1).astype(jnp.bfloat16)
    arrived = lax.all_to_all(panels, "seq", split_axis=0, concat_axis=0, tiled=True)
    flat_rows = arrived.reshape(-1, model_width)
    gate = lax.dot_general(
        flat_rows, w_gate, (((1,), (1,)), ((), ())), preferred_element_type=jnp.float32
    )
    upward = lax.dot_general(
        flat_rows, w_up, (((1,), (1,)), ((), ())), preferred_element_type=jnp.float32
    )
    hidden = (jax.nn.silu(gate) * upward).astype(jnp.bfloat16)
    result = jnp.dot(hidden, w_down, preferred_element_type=jnp.float32).astype(jnp.bfloat16)
    expert_out = result.reshape(arrived.shape[0], arrived.shape[1], model_width)
    returned = lax.all_to_all(expert_out, "seq", split_axis=0, concat_axis=0, tiled=True)
    moe_terms = jnp.dot(
        combine, returned.reshape(-1, model_width), preferred_element_type=jnp.float32
    )
    moe_rows = lax.psum_scatter(moe_terms, "ep", scatter_dimension=0, tiled=True)
    return (resid_rows + moe_rows).astype(jnp.bfloat16)


def solution(mesh):
    in_specs = (
        P("seq", None),
        P(),
        P(None, "ep"),
        P(None, "ep"),
        P(None, "ep"),
        P("ep", None),
        P(),
        P("seq", None),
        P("seq", None),
        P(("seq", "ep"), None),
        P(("seq", "ep"), None),
        P(("seq", "ep"), None),
    )
    out_specs = P(("seq", "ep"), None)
    return jax.shard_map(body, mesh=mesh, in_specs=in_specs, out_specs=out_specs, check_vma=False)
```

profile of v0, /device:TPU:0, one launch (start us, length us, event | category | flops | bytes accessed | tf_op | source)
XLA Modules:
  0.0 210.8 jit_solution(13454979332110237027)
XLA Ops:
  6.5 0.0 all-reduce.2.cloned.1.call-start
  6.6 1.3 fusion.5
  8.0 1.6 convolution_convert_fusion.4
  9.6 0.4 convolution_convert_fusion.3
  10.0 6.1 %collective-permute-start = (bf16[2,128,128]{2,1,0:T(8,128)(2,1)S(1)}, bf16[2,128,128]{2,1,0:T(8,128)(2,1)S(1)}, u32[]{:S(2)}, u32[]{:S(2)}) collective-permute-start(bf16[2,128,128]{2,1,0:T(8,128)(2,1)S(1)} %pad_maximum_fusion), channel_id=1, source_target_pairs={{0,16},{4,20},{8,24},{12,28},{1,17},{5,21},{9,25},{13,29},{2,18},{... | collective-permute-start | bytes 196616 | tf_op jit(solution)/shard_map/ppermute | solution.py:15
  16.1 4.4 %collective-permute-start.1 = (bf16[2,128,128]{2,1,0:T(8,128)(2,1)S(1)}, bf16[2,128,128]{2,1,0:T(8,128)(2,1)S(1)}, u32[]{:S(2)}, u32[]{:S(2)}) collective-permute-start(bf16[2,128,128]{2,1,0:T(8,128)(2,1)S(1)} %pad_maximum_fusion), channel_id=1, source_target_pairs={{0,12},{4,16},{8,20},{12,24},{16,28},{1,13},{5,17},{9,21},{13,25},... | collective-permute-start | bytes 196616 | tf_op jit(solution)/shard_map/ppermute | solution.py:15
  20.6 1.3 collective-permute-start.2
  21.9 3.1 %collective-permute-start.3 = (bf16[2,128,128]{2,1,0:T(8,128)(2,1)S(1)}, bf16[2,128,128]{2,1,0:T(8,128)(2,1)S(1)}, u32[]{:S(2)}, u32[]{:S(2)}) collective-permute-start(bf16[2,128,128]{2,1,0:T(8,128)(2,1)S(1)} %pad_maximum_fusion), channel_id=1, source_target_pairs={{0,4},{4,8},{8,12},{12,16},{16,20},{20,24},{24,28},{1,5},{5,9},{9,... | collective-permute-start | bytes 196616 | tf_op jit(solution)/shard_map/ppermute | solution.py:15
  25.0 0.1 fusion.25
  25.3 1.5 collective-permute-done.3
  26.9 0.6 fusion.45
  27.5 0.2 fusion.17
  27.7 1.6 fusion.4
  29.4 0.2 fusion.1
  29.6 35.5 %all-reduce.2.cloned.1.call-done = f32[128,2048]{1,0:T(8,128)} async-done(((f32[128,2048]{1,0:T(8,128)}), f32[128,2048]{1,0:T(8,128)}) %all-reduce.2.cloned.1.call-update) | async-done | bytes 1048592 | tf_op jit(solution)/shard_map/psum | solution.py:79
  65.1 1.4 multiply_reduce_fusion
  66.6 1.0 copy-done.1
  67.6 1.9 convolution_convert_fusion.1
  69.4 1.6 reshape.52
  71.0 47.5 %all_to_all.10 = bf16[8,52,2048]{2,1,0:T(8,128)(2,1)} all-to-all(bf16[8,52,2048]{2,1,0:T(8,128)(2,1)S(1)} %reshape.52), channel_id=1, replica_groups=mesh['seq'=8,'ep'=4] {'seq'}, dimensions={0} | all-to-all | bytes 3407872 | tf_op jit(solution)/shard_map/all_to_all | solution.py:109
  118.6 1.7 reshape.53
  120.3 1.4 fusion.48
  121.7 3.9 %convolution_convert_fusion = bf16[416,2048]{1,0:T(8,128)(2,1)} fusion(bf16[176,2048]{1,0:T(8,128)(2,1)S(1)} %copy-done, bf16[416,2048]{1,0:T(8,128)(2,1)S(1)} %reshape.53, bf16[176,2048]{1,0:T(8,128)(2,1)} %param.22, f32[416,176]{0,1:T(8,128)} %fusion.48), kind=kOutput, calls=%fused_computation | convolution fusion | flops 601076736 | bytes 5142528 | tf_op jit(solution)/shard_map/dot_general | solution.py:118
  125.6 2.6 %reshape.54 = bf16[8,52,2048]{2,1,0:T(8,128)(2,1)} reshape(bf16[416,2048]{1,0:T(8,128)(2,1)} %convolution_convert_fusion) | data formatting | bytes 3407872 | tf_op jit(solution)/shard_map/reshape | solution.py:119
  128.1 3.7 %all-to-all-start.1 = ((bf16[8,52,2048]{2,1,0:T(8,128)(2,1)}), bf16[8,52,2048]{2,1,0:T(8,128)(2,1)S(1)}, u32[]{:S(2)}, u32[]{:S(2)}) async-start(bf16[8,52,2048]{2,1,0:T(8,128)(2,1)} %reshape.54), calls=%async_computation.1 | async-start | bytes 3670016 | tf_op jit(solution)/shard_map/all_to_all | solution.py:120
  131.9 0.0 reduce-scatter.2.cloned.1.call-start
  131.9 0.3 select_reduce_fusion
  132.2 41.7 %all-to-all-done.1 = bf16[8,52,2048]{2,1,0:T(8,128)(2,1)S(1)} async-done(((bf16[8,52,2048]{2,1,0:T(8,128)(2,1)}), bf16[8,52,2048]{2,1,0:T(8,128)(2,1)S(1)}, u32[]{:S(2)}, u32[]{:S(2)}) %all-to-all-start.1) | async-done | bytes 1703968 | tf_op jit(solution)/shard_map/all_to_all | solution.py:120
  174.0 1.4 reshape.55
  175.3 2.9 %fusion.49 = f32[128,2048]{1,0:T(8,128)} fusion(bf16[128,416]{0,1:T(8,128)(2,1)S(1)} %select_reduce_fusion, bf16[416,2048]{1,0:T(8,128)(2,1)} %reshape.55), kind=kOutput, calls=%fused_computation.87 | convolution fusion | flops 218103808 | bytes 2859008 | tf_op jit(solution)/shard_map/dot_general | solution.py:121
  178.3 24.0 %reduce-scatter.2.cloned.1.call-done = f32[32,2048]{1,0:T(8,128)} async-done(((f32[128,2048]{1,0:T(8,128)}), f32[32,2048]{1,0:T(8,128)}) %reduce-scatter.2.cloned.1.call-update) | async-done | bytes 262160 | tf_op jit(solution)/shard_map/reduce_scatter | solution.py:124
  202.3 1.7 add_convert_fusion
  (42 shorter events, 0.3 us)
Async XLA Ops:
  6.5 115.2 %copy-start = (bf16[176,2048]{1,0:T(8,128)(2,1)S(1)}, bf16[176,2048]{1,0:T(8,128)(2,1)}, u32[]{:S(2)}) copy-start(bf16[176,2048]{1,0:T(8,128)(2,1)} %param.23) | copy-start | bytes 2162692
  6.5 3.1 %copy-start.2 = (bf16[128,2048]{1,0:T(8,128)(2,1)S(1)}, bf16[128,2048]{1,0:T(8,128)(2,1)}, u32[]{:S(2)}) copy-start(bf16[128,2048]{1,0:T(8,128)(2,1)} %param.12) | copy-start | bytes 1572868
  6.5 3.1 %copy-start.10 = (f32[2048]{0:T(1024)S(1)}, f32[2048]{0:T(1024)}, u32[]{:S(2)}) copy-start(f32[2048]{0:T(1024)} %param.13) | copy-start | bytes 24580
  6.5 3.1 %copy-start.8 = (bf16[2048,128]{1,0:T(8,128)(2,1)S(1)}, bf16[2048,128]{1,0:T(8,128)(2,1)}, u32[]{:S(2)}) copy-start(bf16[2048,128]{1,0:T(8,128)(2,1)} %param.16) | copy-start | bytes 1572868
  6.5 18.5 %copy-start.4 = (s32[128,6]{0,1:T(8,128)S(1)}, s32[128,6]{0,1:T(8,128)}, u32[]{:S(2)}) copy-start(s32[128,6]{0,1:T(8,128)} %param.19) | copy-start | bytes 9220
  6.5 58.6 %all-reduce.2.cloned.1.call-start = ((), (), s32[]{:S(2)}) async-start(), calls=%async_computation.3 | async-start | bytes 2097152 | tf_op jit(solution)/shard_map/psum | solution.py:79
  8.0 18.9 %copy-start.9 = (bf16[2048,128]{1,0:T(8,128)(2,1)S(1)}, bf16[2048,128]{1,0:T(8,128)(2,1)}, u32[]{:S(2)}) copy-start(bf16[2048,128]{1,0:T(8,128)(2,1)} %param.14) | copy-start | bytes 1572868
  10.0 17.7 %copy-start.3 = (bf16[128,2048]{1,0:T(8,128)(2,1)S(1)}, bf16[128,2048]{1,0:T(8,128)(2,1)}, u32[]{:S(2)}) copy-start(bf16[128,2048]{1,0:T(8,128)(2,1)} %param.17) | copy-start | bytes 1572868
  10.0 15.2 %collective-permute-start = (bf16[2,128,128]{2,1,0:T(8,128)(2,1)S(1)}, bf16[2,128,128]{2,1,0:T(8,128)(2,1)S(1)}, u32[]{:S(2)}, u32[]{:S(2)}) collective-permute-start(bf16[2,128,128]{2,1,0:T(8,128)(2,1)S(1)} %pad_maximum_fusion), channel_id=1, source_target_pairs={{0,16},{4,20},{8,24},{12,28},{1,17},{5,21},{9,25},{13,29},{2,18},{... | collective-permute-start | bytes 196616 | tf_op jit(solution)/shard_map/ppermute | solution.py:15
  16.1 9.1 %collective-permute-start.1 = (bf16[2,128,128]{2,1,0:T(8,128)(2,1)S(1)}, bf16[2,128,128]{2,1,0:T(8,128)(2,1)S(1)}, u32[]{:S(2)}, u32[]{:S(2)}) collective-permute-start(bf16[2,128,128]{2,1,0:T(8,128)(2,1)S(1)} %pad_maximum_fusion), channel_id=1, source_target_pairs={{0,12},{4,16},{8,20},{12,24},{16,28},{1,13},{5,17},{9,21},{13,25},... | collective-permute-start | bytes 196616 | tf_op jit(solution)/shard_map/ppermute | solution.py:15
  20.6 4.7 %collective-permute-start.2 = (bf16[2,128,128]{2,1,0:T(8,128)(2,1)S(1)}, bf16[2,128,128]{2,1,0:T(8,128)(2,1)S(1)}, u32[]{:S(2)}, u32[]{:S(2)}) collective-permute-start(bf16[2,128,128]{2,1,0:T(8,128)(2,1)S(1)} %pad_maximum_fusion), channel_id=1, source_target_pairs={{0,8},{4,12},{8,16},{12,20},{16,24},{20,28},{1,9},{5,13},{9,17},{1... | collective-permute-start | bytes 196616 | tf_op jit(solution)/shard_map/ppermute | solution.py:15
  21.9 5.0 %collective-permute-start.3 = (bf16[2,128,128]{2,1,0:T(8,128)(2,1)S(1)}, bf16[2,128,128]{2,1,0:T(8,128)(2,1)S(1)}, u32[]{:S(2)}, u32[]{:S(2)}) collective-permute-start(bf16[2,128,128]{2,1,0:T(8,128)(2,1)S(1)} %pad_maximum_fusion), channel_id=1, source_target_pairs={{0,4},{4,8},{8,12},{12,16},{16,20},{20,24},{24,28},{1,5},{5,9},{9,... | collective-permute-start | bytes 196616 | tf_op jit(solution)/shard_map/ppermute | solution.py:15
  29.3 38.3 %copy-start.5 = (f32[2048]{0:T(1024)S(1)}, f32[2048]{0:T(1024)}, u32[]{:S(2)}) copy-start(f32[2048]{0:T(1024)} %param.18) | copy-start | bytes 24580
  66.6 1.0 copy-start.1
  118.6 1.7 copy-start.7
  128.1 3.8 %copy-start.6 = (f32[128,6]{0,1:T(8,128)S(1)}, f32[128,6]{0,1:T(8,128)}, u32[]{:S(2)}) copy-start(f32[128,6]{0,1:T(8,128)} %param.20) | copy-start | bytes 9220
  128.1 45.8 %all-to-all-start.1 = ((bf16[8,52,2048]{2,1,0:T(8,128)(2,1)}), bf16[8,52,2048]{2,1,0:T(8,128)(2,1)S(1)}, u32[]{:S(2)}, u32[]{:S(2)}) async-start(bf16[8,52,2048]{2,1,0:T(8,128)(2,1)} %reshape.54), calls=%async_computation.1 | async-start | bytes 3670016 | tf_op jit(solution)/shard_map/all_to_all | solution.py:120
  131.9 70.4 %reduce-scatter.2.cloned.1.call-start = ((), (), s32[]{:S(2)}) async-start(), calls=%async_computation.4 | async-start | bytes 1310720 | tf_op jit(solution)/shard_map/reduce_scatter | solution.py:124
Sparse Core Ops, SparseCore 0:
  29.4 35.6 all-reduce.1
  178.4 23.8 reduce-scatter.1
where the time goes:
time: 211 us
  waiting for transfers between devices  103 us (49%)
  blocking collectives  47.5 us (23%)
  starting transfers between devices  18.7 us (9%)
  matrix products  14.3 us (7%)
  between operations  13.7 us (6%)
  local copies, waits for them, and re-layouts  8.3 us (4%)
  other arithmetic  5.34 us (3%)
    all_to_all x1, blocking collectives, body(): lax.all_to_all(panels, 'seq', split_axis=0, concat_axis=0, tiled=True)  47.5 us
    all_to_all x1, waiting for transfers between devices, body(): lax.all_to_all(expert_out, 'seq', split_axis=0, concat_axis=0, tiled=True)  41.7 us
    psum x1, waiting for transfers between devices, body(): attn_total = lax.psum(head_terms, 'ep')  35.5 us
    reduce_scatter x1, waiting for transfers between devices, body(): lax.psum_scatter(moe_terms, 'ep', scatter_dimension=0, tiled=True)  24 us
    ppermute x4, starting transfers between devices, shifted(): return lax.ppermute(shard, axis, pairs)  14.9 us
  transfers between devices with their start and end apart: 7, of which 4 were waited for; matrix products, arithmetic and copies ran while one was open for 0% of the time, Pallas kernels for 0%

commit v1 on v0

--- a/solution.py
+++ b/solution.py
@@ -3,6 +3,7 @@
 import jax.numpy as jnp
 from jax import lax
 from jax.sharding import PartitionSpec as P
+from jax.lax import all_gather
 
 EXP_ROW = 2
 SPAN = 4
@@ -76,7 +77,8 @@
         attention_probabilities, window_value_rows, preferred_element_type=jnp.float32
     ).astype(jnp.bfloat16)
     head_terms = jnp.dot(attention_output, w_out, preferred_element_type=jnp.float32)
-    attn_total = lax.psum(head_terms, "ep")
+    pass_ticks_here = lambda sample: jnp.sum(all_gather(sample, axis_name="ep"), axis=0)
+    attn_total = pass_ticks_here(head_terms)
     residual = tok_float + attn_total
     moe_in = root_norm(residual, moe_gain).astype(jnp.bfloat16)
     resid_rows = lax.dynamic_slice_in_dim(residual, ep_place * row_share, row_share, 0)

time: 211 us -> 211 us (level)
    psum x1 -> x0, waiting for transfers between devices: 35.5 us -> none  [body(): attn_total = lax.psum(head_terms, 'ep')]
    all_gather x0 -> x1, waiting for transfers between devices: none -> 33.5 us  [body(): all_gather(sample, axis_name='ep')]
    reduce_sum x0 -> x1, other arithmetic: none -> 2.6 us  [body(): jnp.sum(all_gather(sample, axis_name='ep'), axis=0)]
where the time goes in v1:
time: 211 us
  waiting for transfers between devices  101 us (48%)
  blocking collectives  48.4 us (23%)
  starting transfers between devices  18.7 us (9%)
  matrix products  14.3 us (7%)
  between operations  13.7 us (6%)
  local copies, waits for them, and re-layouts  8.31 us (4%)
  other arithmetic  6.77 us (3%)
    all_to_all x1, blocking collectives, body(): lax.all_to_all(panels, 'seq', split_axis=0, concat_axis=0, tiled=True)  48.4 us
    all_to_all x1, waiting for transfers between devices, body(): lax.all_to_all(expert_out, 'seq', split_axis=0, concat_axis=0, tiled=True)  42.2 us
    all_gather x1, waiting for transfers between devices, body(): all_gather(sample, axis_name='ep')  33.5 us
    reduce_scatter x1, waiting for transfers between devices, body(): lax.psum_scatter(moe_terms, 'ep', scatter_dimension=0, tiled=True)  23.1 us
    ppermute x4, starting transfers between devices, shifted(): return lax.ppermute(shard, axis, pairs)  14.9 us
  transfers between devices with their start and end apart: 7, of which 4 were waited for; matrix products, arithmetic and copies ran while one was open for 0% of the time, Pallas kernels for 0%

profile of v1, /device:TPU:0, one launch (start us, length us, event | category | flops | bytes accessed | tf_op | source)
XLA Modules:
  0.0 210.8 jit_solution(2641358039041187021)
XLA Ops:
  6.6 1.4 fusion.5
  8.0 1.6 convolution_convert_fusion.4
  9.6 0.4 convolution_convert_fusion.3
  10.0 6.1 %collective-permute-start = (bf16[2,128,128]{2,1,0:T(8,128)(2,1)S(1)}, bf16[2,128,128]{2,1,0:T(8,128)(2,1)S(1)}, u32[]{:S(2)}, u32[]{:S(2)}) collective-permute-start(bf16[2,128,128]{2,1,0:T(8,128)(2,1)S(1)} %pad_maximum_fusion), channel_id=1, source_target_pairs={{0,16},{4,20},{8,24},{12,28},{1,17},{5,21},{9,25},{13,29},{2,18},{... | collective-permute-start | bytes 196616 | tf_op jit(solution)/shard_map/ppermute | solution.py:16
  16.1 4.4 %collective-permute-start.1 = (bf16[2,128,128]{2,1,0:T(8,128)(2,1)S(1)}, bf16[2,128,128]{2,1,0:T(8,128)(2,1)S(1)}, u32[]{:S(2)}, u32[]{:S(2)}) collective-permute-start(bf16[2,128,128]{2,1,0:T(8,128)(2,1)S(1)} %pad_maximum_fusion), channel_id=1, source_target_pairs={{0,12},{4,16},{8,20},{12,24},{16,28},{1,13},{5,17},{9,21},{13,25},... | collective-permute-start | bytes 196616 | tf_op jit(solution)/shard_map/ppermute | solution.py:16
  20.5 1.3 collective-permute-start.2
  21.8 3.1 %collective-permute-start.3 = (bf16[2,128,128]{2,1,0:T(8,128)(2,1)S(1)}, bf16[2,128,128]{2,1,0:T(8,128)(2,1)S(1)}, u32[]{:S(2)}, u32[]{:S(2)}) collective-permute-start(bf16[2,128,128]{2,1,0:T(8,128)(2,1)S(1)} %pad_maximum_fusion), channel_id=1, source_target_pairs={{0,4},{4,8},{8,12},{12,16},{16,20},{20,24},{24,28},{1,5},{5,9},{9,... | collective-permute-start | bytes 196616 | tf_op jit(solution)/shard_map/ppermute | solution.py:16
  25.1 1.8 collective-permute-done.3
  26.9 0.6 fusion.45
  27.5 0.2 fusion.17
  27.7 1.5 fusion.4
  29.3 0.1 fusion.25
  29.4 0.1 select_reduce_fusion.1
  29.5 0.2 fusion.1
  29.8 33.5 %all-gather.3.cloned.1.call-done = f32[512,2048]{1,0:T(8,128)} async-done(((f32[128,2048]{1,0:T(8,128)}), f32[512,2048]{1,0:T(8,128)}) %all-gather.3.cloned.1.call-update) | async-done | bytes 4194320 | tf_op jit(solution)/shard_map/all_gather | solution.py:80
  63.2 2.6 %reduce_sum.65 = f32[128,2048]{1,0:T(8,128)S(1)} reduce(f32[4,128,2048]{2,1,0:T(8,128)} %bitcast.50, f32[]{:T(128)} %constant.64.clone.1), dimensions={0}, to_apply=%region_3.4 | reduce | flops 786432 | bytes 5242884 | tf_op jit(solution)/shard_map/reduce_sum | solution.py:80
  65.8 0.2 multiply_reduce_fusion
  66.1 1.0 copy-done.1
  67.0 1.9 convolution_convert_fusion.1
  68.9 1.6 reshape.52
  70.5 48.4 %all_to_all.10 = bf16[8,52,2048]{2,1,0:T(8,128)(2,1)} all-to-all(bf16[8,52,2048]{2,1,0:T(8,128)(2,1)S(1)} %reshape.52), channel_id=1, replica_groups=mesh['seq'=8,'ep'=4] {'seq'}, dimensions={0} | all-to-all | bytes 3407872 | tf_op jit(solution)/shard_map/all_to_all | solution.py:111
  118.9 1.7 reshape.53
  120.6 1.4 fusion.48
  122.0 3.9 %convolution_convert_fusion = bf16[416,2048]{1,0:T(8,128)(2,1)} fusion(bf16[176,2048]{1,0:T(8,128)(2,1)S(1)} %copy-done, bf16[416,2048]{1,0:T(8,128)(2,1)S(1)} %reshape.53, bf16[176,2048]{1,0:T(8,128)(2,1)} %param.22, f32[416,176]{0,1:T(8,128)} %fusion.48), kind=kOutput, calls=%fused_computation | convolution fusion | flops 601076736 | bytes 5142528 | tf_op jit(solution)/shard_map/dot_general | solution.py:120
  125.9 2.6 %reshape.54 = bf16[8,52,2048]{2,1,0:T(8,128)(2,1)} reshape(bf16[416,2048]{1,0:T(8,128)(2,1)} %convolution_convert_fusion) | data formatting | bytes 3407872 | tf_op jit(solution)/shard_map/reshape | solution.py:121
  128.5 3.8 %all-to-all-start.1 = ((bf16[8,52,2048]{2,1,0:T(8,128)(2,1)}), bf16[8,52,2048]{2,1,0:T(8,128)(2,1)S(1)}, u32[]{:S(2)}, u32[]{:S(2)}) async-start(bf16[8,52,2048]{2,1,0:T(8,128)(2,1)} %reshape.54), calls=%async_computation.1 | async-start | bytes 3670016 | tf_op jit(solution)/shard_map/all_to_all | solution.py:122
  132.3 0.3 select_reduce_fusion
  132.6 42.2 %all-to-all-done.1 = bf16[8,52,2048]{2,1,0:T(8,128)(2,1)S(1)} async-done(((bf16[8,52,2048]{2,1,0:T(8,128)(2,1)}), bf16[8,52,2048]{2,1,0:T(8,128)(2,1)S(1)}, u32[]{:S(2)}, u32[]{:S(2)}) %all-to-all-start.1) | async-done | bytes 1703968 | tf_op jit(solution)/shard_map/all_to_all | solution.py:122
  174.8 1.4 reshape.55
  176.2 2.9 %fusion.49 = f32[128,2048]{1,0:T(8,128)} fusion(bf16[128,416]{0,1:T(8,128)(2,1)S(1)} %select_reduce_fusion, bf16[416,2048]{1,0:T(8,128)(2,1)} %reshape.55), kind=kOutput, calls=%fused_computation.87 | convolution fusion | flops 218103808 | bytes 2859008 | tf_op jit(solution)/shard_map/dot_general | solution.py:123
  179.1 23.1 %reduce-scatter.2.cloned.1.call-done = f32[32,2048]{1,0:T(8,128)} async-done(((f32[128,2048]{1,0:T(8,128)}), f32[32,2048]{1,0:T(8,128)}) %reduce-scatter.2.cloned.1.call-update) | async-done | bytes 262160 | tf_op jit(solution)/shard_map/reduce_scatter | solution.py:126
  202.2 1.7 add_convert_fusion
  (43 shorter events, 0.3 us)
Async XLA Ops:
  6.5 115.5 %copy-start = (bf16[176,2048]{1,0:T(8,128)(2,1)S(1)}, bf16[176,2048]{1,0:T(8,128)(2,1)}, u32[]{:S(2)}) copy-start(bf16[176,2048]{1,0:T(8,128)(2,1)} %param.23) | copy-start | bytes 2162692
  6.5 3.1 %copy-start.2 = (bf16[128,2048]{1,0:T(8,128)(2,1)S(1)}, bf16[128,2048]{1,0:T(8,128)(2,1)}, u32[]{:S(2)}) copy-start(bf16[128,2048]{1,0:T(8,128)(2,1)} %param.12) | copy-start | bytes 1572868
  6.5 3.1 %copy-start.10 = (f32[2048]{0:T(1024)S(1)}, f32[2048]{0:T(1024)}, u32[]{:S(2)}) copy-start(f32[2048]{0:T(1024)} %param.13) | copy-start | bytes 24580
  6.5 3.1 %copy-start.8 = (bf16[2048,128]{1,0:T(8,128)(2,1)S(1)}, bf16[2048,128]{1,0:T(8,128)(2,1)}, u32[]{:S(2)}) copy-start(bf16[2048,128]{1,0:T(8,128)(2,1)} %param.16) | copy-start | bytes 1572868
  6.5 56.7 %all-gather.3.cloned.1.call-start = ((), (), s32[]{:S(2)}) async-start(), calls=%async_computation.4 | async-start | bytes 5242880 | tf_op jit(solution)/shard_map/all_gather | solution.py:80
  7.9 18.9 %copy-start.9 = (bf16[2048,128]{1,0:T(8,128)(2,1)S(1)}, bf16[2048,128]{1,0:T(8,128)(2,1)}, u32[]{:S(2)}) copy-start(bf16[2048,128]{1,0:T(8,128)(2,1)} %param.14) | copy-start | bytes 1572868
  10.0 17.7 %copy-start.3 = (bf16[128,2048]{1,0:T(8,128)(2,1)S(1)}, bf16[128,2048]{1,0:T(8,128)(2,1)}, u32[]{:S(2)}) copy-start(bf16[128,2048]{1,0:T(8,128)(2,1)} %param.17) | copy-start | bytes 1572868
  10.0 15.0 %collective-permute-start = (bf16[2,128,128]{2,1,0:T(8,128)(2,1)S(1)}, bf16[2,128,128]{2,1,0:T(8,128)(2,1)S(1)}, u32[]{:S(2)}, u32[]{:S(2)}) collective-permute-start(bf16[2,128,128]{2,1,0:T(8,128)(2,1)S(1)} %pad_maximum_fusion), channel_id=1, source_target_pairs={{0,16},{4,20},{8,24},{12,28},{1,17},{5,21},{9,25},{13,29},{2,18},{... | collective-permute-start | bytes 196616 | tf_op jit(solution)/shard_map/ppermute | solution.py:16
  16.1 8.9 %collective-permute-start.1 = (bf16[2,128,128]{2,1,0:T(8,128)(2,1)S(1)}, bf16[2,128,128]{2,1,0:T(8,128)(2,1)S(1)}, u32[]{:S(2)}, u32[]{:S(2)}) collective-permute-start(bf16[2,128,128]{2,1,0:T(8,128)(2,1)S(1)} %pad_maximum_fusion), channel_id=1, source_target_pairs={{0,12},{4,16},{8,20},{12,24},{16,28},{1,13},{5,17},{9,21},{13,25},... | collective-permute-start | bytes 196616 | tf_op jit(solution)/shard_map/ppermute | solution.py:16
  20.5 4.5 %collective-permute-start.2 = (bf16[2,128,128]{2,1,0:T(8,128)(2,1)S(1)}, bf16[2,128,128]{2,1,0:T(8,128)(2,1)S(1)}, u32[]{:S(2)}, u32[]{:S(2)}) collective-permute-start(bf16[2,128,128]{2,1,0:T(8,128)(2,1)S(1)} %pad_maximum_fusion), channel_id=1, source_target_pairs={{0,8},{4,12},{8,16},{12,20},{16,24},{20,28},{1,9},{5,13},{9,17},{1... | collective-permute-start | bytes 196616 | tf_op jit(solution)/shard_map/ppermute | solution.py:16
  21.8 5.0 %collective-permute-start.3 = (bf16[2,128,128]{2,1,0:T(8,128)(2,1)S(1)}, bf16[2,128,128]{2,1,0:T(8,128)(2,1)S(1)}, u32[]{:S(2)}, u32[]{:S(2)}) collective-permute-start(bf16[2,128,128]{2,1,0:T(8,128)(2,1)S(1)} %pad_maximum_fusion), channel_id=1, source_target_pairs={{0,4},{4,8},{8,12},{12,16},{16,20},{20,24},{24,28},{1,5},{5,9},{9,... | collective-permute-start | bytes 196616 | tf_op jit(solution)/shard_map/ppermute | solution.py:16
  27.5 1.8 copy-start.4
  65.8 1.2 copy-start.5
  66.1 1.0 copy-start.1
  118.9 1.7 copy-start.7
  128.5 3.8 %copy-start.6 = (f32[128,6]{0,1:T(8,128)S(1)}, f32[128,6]{0,1:T(8,128)}, u32[]{:S(2)}) copy-start(f32[128,6]{0,1:T(8,128)} %param.20) | copy-start | bytes 9220
  128.5 46.4 %all-to-all-start.1 = ((bf16[8,52,2048]{2,1,0:T(8,128)(2,1)}), bf16[8,52,2048]{2,1,0:T(8,128)(2,1)S(1)}, u32[]{:S(2)}, u32[]{:S(2)}) async-start(bf16[8,52,2048]{2,1,0:T(8,128)(2,1)} %reshape.54), calls=%async_computation.1 | async-start | bytes 3670016 | tf_op jit(solution)/shard_map/all_to_all | solution.py:122
  132.2 70.0 %reduce-scatter.2.cloned.1.call-start = ((), (), s32[]{:S(2)}) async-start(), calls=%async_computation.3 | async-start | bytes 1310720 | tf_op jit(solution)/shard_map/reduce_scatter | solution.py:126
Sparse Core Ops, SparseCore 0:
  29.4 33.8 all-gather.2
  179.2 22.9 reduce-scatter.1
